TPU v7x, 32 devices: a whole 2x2x4 slice. The times are simulated.
32 devices in a mesh: rows: 2 (over x), gr: 4 (over z), gc: 4 (over y, core).
Axes of the slice: x: 2, y: 2, z: 4, core: 2. Of those that a mesh axis runs over, the one named last changes fastest.
Arguments:
- tokens: bfloat16 [32768, 768], P(('rows', 'gr', 'gc')), may hold values from -6 to 6
- boxes: int32 [4, 32768], P(None, ('rows', 'gr', 'gc')), may hold values from 0 to 1000
- page_ids: int32 [64, 512], P(('rows', 'gr', 'gc')), may hold values from 0 to 3, never falling along the last dimension, each value on 1 to 256 neighbouring positions
- seg_ids: int32 [64, 512], P(('rows', 'gr', 'gc')), may hold values from 0 to 63, never falling along the last dimension, each value on 1 to 24 neighbouring positions
- pair_mask: int32 [2, 2048, 2048], P('rows', 'gr', 'gc'), may hold values 0 or 1
- ln1_gain: float32 [768], replicated, may hold values from 0.5 to 1.5
- ln1_bias: float32 [768], replicated, may hold values from -3 to 3
- query_key_value_weight: bfloat16 [768, 2304], replicated, may hold values from -0.21875 to 0.21875
- attention_output_weight: bfloat16 [768, 768], replicated, may hold values from -0.625 to 0.625
- ln2_gain: float32 [768], replicated, may hold values from 0.5 to 1.5
- ln2_bias: float32 [768], replicated, may hold values from -3 to 3
- up_projection_weight: bfloat16 [768, 3072], replicated, may hold values from -0.21875 to 0.21875
- up_projection_bias: float32 [3072], replicated, may hold values from -3 to 3
- down_projection_weight: bfloat16 [3072, 768], replicated, may hold values from -0.15625 to 0.15625
- box_table: float32 [12, 128], replicated, may hold values from -3 to 3
- rel_left: bfloat16 [768, 768], replicated, may hold values from -0.21875 to 0.21875
- rel_right: bfloat16 [768, 768], replicated, may hold values from -0.21875 to 0.21875
- cot_out: bfloat16 [32768, 768], P(('rows', 'gr', 'gc')), may hold values from -6 to 6
- cot_logits: bfloat16 [2, 2048, 2048], P('rows', 'gr', 'gc'), may hold values from -6 to 6
Outputs:
- layer_out: bfloat16 [32768, 768], P(('rows', 'gr', 'gc'))
- pair_logits: float32 [2, 2048, 2048], P('rows', 'gr', 'gc')
- grad_tokens: float32 [32768, 768], P(('rows', 'gr', 'gc'))
- grad_ln1_gain: float32 [768], replicated
- grad_ln1_bias: float32 [768], replicated
- grad_qkv: float32 [1769472], P(('rows', 'gr', 'gc'))
- grad_out_weight: float32 [589824], P(('rows', 'gr', 'gc'))
- grad_ln2_gain: float32 [768], replicated
- grad_ln2_bias: float32 [768], replicated
- grad_up: float32 [2359296], P(('rows', 'gr', 'gc'))
- grad_up_bias: float32 [3072], replicated
- grad_down: float32 [2359296], P(('rows', 'gr', 'gc'))
- grad_box_table: float32 [12, 128], replicated
- grad_rel_left: float32 [589824], P(('rows', 'gr', 'gc'))
- grad_rel_right: float32 [589824], P(('rows', 'gr', 'gc'))
Inputs may be any that keep to these rules, and one draw needn't show every extreme that they name: `page_ids`: within a packed row page ids never fall; each of the 4 pages has 1 to 256 tokens. `seg_ids`: within a packed row segment slots never fall; each of the 64 slots has 1 to 24 tokens.
All inputs are finite; a program needn't handle non-finite values. No bound on the sum of `pair_mask` on one device may be relied on, other than what follows from the above.
Results may differ from a plain program's by a relative error of at most 0.03.
Values may be sent and summed in bfloat16 or wider, within the bound.
A program may use at most 192 MiB of HBM per device.

v0:
```python
import math

import jax
import jax.numpy as jnp
from jax import lax
from jax.sharding import PartitionSpec as P

COORD = 1000
SEG = 64


EPSILON = 1e-05


def norm_fn(values_in, norm_gain, norm_bias):
    average = jnp.mean(values_in, axis=-1, keepdims=True)
    centred = values_in - average
    variance = jnp.mean(centred * centred, axis=-1, keepdims=True)
    return centred * lax.rsqrt(variance + EPSILON) * norm_gain + norm_bias


def exact_gelu(values_in):
    return jax.nn.gelu(values_in, approximate=False)


def bucket_onehot(box_rows, bucket_half):
    centre_x = (box_rows[0] + box_rows[2]) // 2
    centre_y = (box_rows[1] + box_rows[3]) // 2
    bucket_span = 2 * COORD + 1
    bucket_x = (centre_x[None, :] - centre_x[:, None] + COORD) * bucket_half // bucket_span
    bucket_y = (
        centre_y[None, :] - centre_y[:, None] + COORD
    ) * bucket_half // bucket_span + bucket_half
    bucket_ids = lax.iota(jnp.int32, 2 * bucket_half)
    return ((bucket_x[:, :, None] == bucket_ids) | (bucket_y[:, :, None] == bucket_ids)).astype(
        jnp.bfloat16
    )


def split_parts(values_in):
    high_part = values_in.astype(jnp.bfloat16)
    low_part = (values_in - high_part.astype(jnp.float32)).astype(jnp.bfloat16)
    return (high_part, low_part)


def head_scores(projected_rows, box_rows, page_rows, box_table):
    length = projected_rows.shape[0]
    head_count = box_table.shape[0]
    features = projected_rows.shape[1] // 3
    split_heads = projected_rows.reshape(length, 3, head_count, features // head_count)
    queries, key_rows, value_rows = (split_heads[:, 0], split_heads[:, 1], split_heads[:, 2])
    products = jnp.einsum("ihc,jhc->hij", queries, key_rows, preferred_element_type=jnp.float32)
    segment_members = bucket_onehot(box_rows, box_table.shape[1] // 2)
    table_high, table_low = split_parts(box_table)
    box_bias = jnp.einsum(
        "ijb,hb->hij", segment_members, table_high, preferred_element_type=jnp.float32
    )
    box_bias = box_bias + jnp.einsum(
        "ijb,hb->hij", segment_members, table_low, preferred_element_type=jnp.float32
    )
    same_page = page_rows[:, None] == page_rows[None, :]
    head_scale = 1.0 / math.sqrt(features // head_count)
    scores = jnp.where(same_page[None], products * head_scale + box_bias, -1e30)
    return (scores, segment_members, queries, key_rows, value_rows, head_scale)


def attend_one(block_item, box_table):
    projected_rows, box_rows, page_rows = block_item
    scores, segment_members, queries, key_rows, value_rows, head_scale = head_scores(
        projected_rows, box_rows, page_rows, box_table
    )
    highest = jnp.max(scores, axis=-1, keepdims=True)
    shifted = jnp.exp(scores - highest)
    totals = jnp.sum(shifted, axis=-1, keepdims=True)
    softmax_out = (shifted / totals).astype(jnp.bfloat16)
    attended_context = jnp.einsum(
        "hij,jhc->ihc", softmax_out, value_rows, preferred_element_type=jnp.float32
    )
    attended_context = attended_context.reshape(projected_rows.shape[0], -1).astype(jnp.bfloat16)
    return (attended_context, highest[..., 0] + jnp.log(totals[..., 0]))


def attend_back(block_item, box_table):
    projected_rows, box_rows, page_rows, log_total, grad_context = block_item
    scores, segment_members, queries, key_rows, value_rows, head_scale = head_scores(
        projected_rows, box_rows, page_rows, box_table
    )
    length = projected_rows.shape[0]
    softmax_full = jnp.exp(scores - log_total[..., None])
    grad_heads = grad_context.reshape(length, box_table.shape[0], -1)
    grad_probs = jnp.einsum(
        "ihc,jhc->hij", grad_heads, value_rows, preferred_element_type=jnp.float32
    )
    grad_value = jnp.einsum(
        "hij,ihc->jhc",
        softmax_full.astype(jnp.bfloat16),
        grad_heads,
        preferred_element_type=jnp.float32,
    )
    grad_scores = softmax_full * (
        grad_probs - jnp.sum(softmax_full * grad_probs, axis=-1, keepdims=True)
    )
    grad_high, grad_low = split_parts(grad_scores)
    grad_table = jnp.einsum(
        "hij,ijb->hb", grad_high, segment_members, preferred_element_type=jnp.float32
    )
    grad_table = grad_table + jnp.einsum(
        "hij,ijb->hb", grad_low, segment_members, preferred_element_type=jnp.float32
    )
    grad_products = (grad_scores * head_scale).astype(jnp.bfloat16)
    grad_query = jnp.einsum(
        "hij,jhc->ihc", grad_products, key_rows, preferred_element_type=jnp.float32
    )
    grad_key = jnp.einsum(
        "hij,ihc->jhc", grad_products, queries, preferred_element_type=jnp.float32
    )
    grad_rows = (
        jnp.stack((grad_query, grad_key, grad_value), axis=1)
        .reshape(length, -1)
        .astype(jnp.bfloat16)
    )
    return (grad_rows, grad_table)


def body(
    tokens,
    boxes,
    page_ids,
    seg_ids,
    pair_mask,
    ln1_gain,
    ln1_bias,
    query_key_value_weight,
    attention_output_weight,
    ln2_gain,
    ln2_bias,
    up_projection_weight,
    up_projection_bias,
    down_projection_weight,
    box_table,
    rel_left,
    rel_right,
    cot_out,
    cot_logits,
):
    sequences, length = page_ids.shape
    features = tokens.shape[1]
    layer_inputs = tokens.astype(jnp.float32)
    first_norm_output, first_back = jax.vjp(norm_fn, layer_inputs, ln1_gain, ln1_bias)
    first_norm_output = first_norm_output.astype(jnp.bfloat16)
    projected_rows = jnp.dot(
        first_norm_output, query_key_value_weight, preferred_element_type=jnp.float32
    ).astype(jnp.bfloat16)
    projected_seq = projected_rows.reshape(sequences, length, 3 * features)
    box_seq = jnp.transpose(boxes.reshape(4, sequences, length), (1, 0, 2))
    attended_context, log_total = lax.map(
        lambda block_item: attend_one(block_item, box_table), (projected_seq, box_seq, page_ids)
    )
    attended_context = attended_context.reshape(sequences * length, features)
    residual_stream = layer_inputs + jnp.dot(
        attended_context, attention_output_weight, preferred_element_type=jnp.float32
    )
    second_norm_output, second_back = jax.vjp(norm_fn, residual_stream, ln2_gain, ln2_bias)
    second_norm_output = second_norm_output.astype(jnp.bfloat16)
    hidden_input_rows = (
        jnp.dot(second_norm_output, up_projection_weight, preferred_element_type=jnp.float32)
        + up_projection_bias
    )
    activated_hidden, gelu_back = jax.vjp(exact_gelu, hidden_input_rows)
    activated_hidden = activated_hidden.astype(jnp.bfloat16)
    layer_full = residual_stream + jnp.dot(
        activated_hidden, down_projection_weight, preferred_element_type=jnp.float32
    )
    layer_out = layer_full.astype(jnp.bfloat16)
    member_mask = seg_ids[:, None, :] == lax.iota(jnp.int32, SEG)[None, :, None]
    segment_members = member_mask.astype(jnp.bfloat16)
    counts = jnp.sum(member_mask.astype(jnp.float32), axis=2)
    pooled = (
        jnp.einsum(
            "yzw,ywo->yzo",
            segment_members,
            layer_out.reshape(sequences, length, features),
            preferred_element_type=jnp.float32,
        )
        / counts[:, :, None]
    )
    embedded = pooled.reshape(sequences * SEG, features).astype(jnp.bfloat16)
    left_seg = jnp.dot(embedded, rel_left, preferred_element_type=jnp.float32).astype(jnp.bfloat16)
    right_seg = jnp.dot(embedded, rel_right, preferred_element_type=jnp.float32).astype(
        jnp.bfloat16
    )
    row_side = lax.all_gather(left_seg, "gc", axis=0, tiled=True)
    col_side = lax.all_gather(right_seg, "gr", axis=0, tiled=True)
    pair_scale = 1.0 / math.sqrt(rel_left.shape[1])
    pair_keep = pair_mask[0].astype(jnp.float32)
    pair_logits = (
        pair_keep
        * jnp.einsum("ae,be->ab", row_side, col_side, preferred_element_type=jnp.float32)
        * pair_scale
    )
    grad_tile = (cot_logits[0].astype(jnp.float32) * pair_scale * pair_keep).astype(jnp.bfloat16)
    grad_left_seg = lax.psum_scatter(
        jnp.dot(grad_tile, col_side, preferred_element_type=jnp.float32).astype(jnp.bfloat16),
        "gc",
        scatter_dimension=0,
        tiled=True,
    )
    grad_right_seg = lax.psum_scatter(
        jnp.einsum("ab,ae->be", grad_tile, row_side, preferred_element_type=jnp.float32).astype(
            jnp.bfloat16
        ),
        "gr",
        scatter_dimension=0,
        tiled=True,
    )
    grad_rel_left = jnp.einsum(
        "sd,se->de", embedded, grad_left_seg, preferred_element_type=jnp.float32
    )
    grad_rel_right = jnp.einsum(
        "sd,se->de", embedded, grad_right_seg, preferred_element_type=jnp.float32
    )
    grad_embedded = jnp.einsum(
        "se,de->sd", grad_left_seg, rel_left, preferred_element_type=jnp.float32
    )
    grad_embedded = grad_embedded + jnp.einsum(
        "se,de->sd", grad_right_seg, rel_right, preferred_element_type=jnp.float32
    )
    pooled_gradient = grad_embedded.reshape(sequences, SEG, features) / counts[:, :, None]
    spread_back = jnp.take_along_axis(pooled_gradient, seg_ids[:, :, None], axis=1)
    grad_final = cot_out.astype(jnp.float32) + spread_back.reshape(sequences * length, features)
    grad_branch = grad_final.astype(jnp.bfloat16)
    grad_down = jnp.einsum(
        "tf,td->fd", activated_hidden, grad_branch, preferred_element_type=jnp.float32
    )
    grad_active = jnp.einsum(
        "td,fd->tf", grad_branch, down_projection_weight, preferred_element_type=jnp.float32
    )
    grad_hidden = gelu_back(grad_active)[0].astype(jnp.bfloat16)
    grad_up_bias = jnp.sum(grad_hidden.astype(jnp.float32), axis=0)
    grad_up = jnp.einsum(
        "td,tf->df", second_norm_output, grad_hidden, preferred_element_type=jnp.float32
    )
    grad_second = jnp.einsum(
        "tf,df->td", grad_hidden, up_projection_weight, preferred_element_type=jnp.float32
    )
    grad_resid_norm, grad_ln2_gain, grad_ln2_bias = second_back(grad_second)
    grad_resid = grad_final + grad_resid_norm
    grad_attn = grad_resid.astype(jnp.bfloat16)
    grad_out = jnp.einsum(
        "td,te->de", attended_context, grad_attn, preferred_element_type=jnp.float32
    )
    grad_context = jnp.einsum(
        "te,de->td", grad_attn, attention_output_weight, preferred_element_type=jnp.float32
    ).astype(jnp.bfloat16)
    grad_rows, grad_tables = lax.map(
        lambda block_item: attend_back(block_item, box_table),
        (
            projected_seq,
            box_seq,
            page_ids,
            log_total,
            grad_context.reshape(sequences, length, features),
        ),
    )
    grad_rows = grad_rows.reshape(sequences * length, 3 * features)
    grad_table = jnp.sum(grad_tables, axis=0)
    grad_qkv = jnp.einsum(
        "td,te->de", first_norm_output, grad_rows, preferred_element_type=jnp.float32
    )
    grad_first = jnp.einsum(
        "te,de->td", grad_rows, query_key_value_weight, preferred_element_type=jnp.float32
    )
    grad_input_norm, grad_ln1_gain, grad_ln1_bias = first_back(grad_first)
    grad_tokens = grad_resid + grad_input_norm
    small_sums = lax.psum(
        (grad_ln1_gain, grad_ln1_bias, grad_ln2_gain, grad_ln2_bias, grad_up_bias, grad_table),
        ("rows", "gr", "gc"),
    )
    qkv_share, out_share, up_share, down_share, left_share, right_share = (
        lax.psum_scatter(
            grad_qkv.reshape(-1), ("rows", "gr", "gc"), scatter_dimension=0, tiled=True
        ),
        lax.psum_scatter(
            grad_out.reshape(-1), ("rows", "gr", "gc"), scatter_dimension=0, tiled=True
        ),
        lax.psum_scatter(
            grad_up.reshape(-1), ("rows", "gr", "gc"), scatter_dimension=0, tiled=True
        ),
        lax.psum_scatter(
            grad_down.reshape(-1), ("rows", "gr", "gc"), scatter_dimension=0, tiled=True
        ),
        lax.psum_scatter(
            grad_rel_left.reshape(-1), ("rows", "gr", "gc"), scatter_dimension=0, tiled=True
        ),
        lax.psum_scatter(
            grad_rel_right.reshape(-1), ("rows", "gr", "gc"), scatter_dimension=0, tiled=True
        ),
    )
    return (
        layer_out,
        pair_logits[None],
        grad_tokens,
        small_sums[0],
        small_sums[1],
        qkv_share,
        out_share,
        small_sums[2],
        small_sums[3],
        up_share,
        small_sums[4],
        down_share,
        small_sums[5],
        left_share,
        right_share,
    )


def solution(mesh):
    in_specs = (
        P(("rows", "gr", "gc"), None),
        P(None, ("rows", "gr", "gc")),
        P(("rows", "gr", "gc"), None),
        P(("rows", "gr", "gc"), None),
        P("rows", "gr", "gc"),
        P(),
        P(),
        P(),
        P(),
        P(),
        P(),
        P(),
        P(),
        P(),
        P(),
        P(),
        P(),
        P(("rows", "gr", "gc"), None),
        P("rows", "gr", "gc"),
    )
    out_specs = (
        P(("rows", "gr", "gc"), None),
        P("rows", "gr", "gc"),
        P(("rows", "gr", "gc"), None),
        P(),
        P(),
        P(("rows", "gr", "gc")),
        P(("rows", "gr", "gc")),
        P(),
        P(),
        P(("rows", "gr", "gc")),
        P(),
        P(("rows", "gr", "gc")),
        P(),
        P(("rows", "gr", "gc")),
        P(("rows", "gr", "gc")),
    )
    return jax.shard_map(body, mesh=mesh, in_specs=in_specs, out_specs=out_specs, check_vma=False)
```

profile of v0, /device:TPU:0, one launch (start us, length us, event | category | flops | bytes accessed | tf_op | source)
XLA Modules:
  0.0 2701.6 jit_solution(3124508905152207875)
XLA Ops:
  27.6 630.0 %while.30 = (s32[]{:T(128)}, bf16[2,512,768]{2,1,0:T(8,128)(2,1)}, f32[2,12,512]{2,1,0:T(8,128)}, bf16[2,512,2304]{1,2,0:T(8,128)(2,1)}, s32[2,512]{1,0:T(2,128)...) while((s32[]{:T(128)}, bf16[2,512,768]{2,1,0:T(8,128)(2,1)}, ...), condition=%wide.region_5.6_spmd, body=%wide.region_2.5_spmd.sunk | while | flops 2655402496 | bytes 224872848 | solution.py:156
  30.5 120.0 %fusion.254 = f32[12,512,512]{2,0,1:T(8,128)} fusion(s32[512,512]{1,0:T(8,128)S(1)} %fusion.253, s32[512,512]{1,0:T(8,128)S(1)} %add_select_fusion.13, f32[12,128]{1,0:T(8,128)} %get-tuple-element.598, bf16[12,128]{1,0:T(8,128)(2,1)} %get-tuple-element.597), kind=kOutput, calls=%fused_computation.4.clone.3 | convolution fusion | flops 905974272 | bytes 14689280 | tf_op jit(solution)/shard_map/while/body/eval_jaxpr/ijb,hb->hij/dot_general | solution.py:58
  150.6 17.8 copy.97
  168.3 120.6 %fusion.255 = f32[512,512,12]{1,2,0:T(8,128)} fusion(s32[512,512]{1,0:T(8,128)} %copy-done.11, s32[512,512]{1,0:T(8,128)} %copy-done.12, bf16[12,128]{1,0:T(8,128)(2,1)} %get-tuple-element.597), kind=kOutput, calls=%fused_computation.5.clone.2 | convolution fusion | flops 905969664 | bytes 14683136 | tf_op jit(solution)/shard_map/while/body/eval_jaxpr/ijb,hb->hij/dot_general | solution.py:55
  345.4 120.0 %fusion.254 = f32[12,512,512]{2,0,1:T(8,128)} fusion(s32[512,512]{1,0:T(8,128)S(1)} %fusion.253, s32[512,512]{1,0:T(8,128)S(1)} %add_select_fusion.13, f32[12,128]{1,0:T(8,128)} %get-tuple-element.598, bf16[12,128]{1,0:T(8,128)(2,1)} %get-tuple-element.597), kind=kOutput, calls=%fused_computation.4.clone.3 | convolution fusion | flops 905974272 | bytes 14689280 | tf_op jit(solution)/shard_map/while/body/eval_jaxpr/ijb,hb->hij/dot_general | solution.py:58
  465.4 17.8 copy.97
  483.1 120.6 %fusion.255 = f32[512,512,12]{1,2,0:T(8,128)} fusion(s32[512,512]{1,0:T(8,128)} %copy-done.11, s32[512,512]{1,0:T(8,128)} %copy-done.12, bf16[12,128]{1,0:T(8,128)(2,1)} %get-tuple-element.597), kind=kOutput, calls=%fused_computation.5.clone.2 | convolution fusion | flops 905969664 | bytes 14683136 | tf_op jit(solution)/shard_map/while/body/eval_jaxpr/ijb,hb->hij/dot_general | solution.py:55
  663.3 34.8 %multiply_convert_fusion.11 = (bf16[1024,3072]{1,0:T(8,128)(2,1)S(1)}, f32[1024,3072]{1,0:T(8,128)}, f32[1024,3072]{1,0:T(8,128)}) fusion(f32[3072]{0:T(1024)S(1)} %copy-done.46, bf16[768,3072]{1,0:T(8,128)(2,1)S(1)} %copy-done.43, f32[1024,768]{1,0:T(8,128)S(1)} %get-tuple-element.425, f32[768]{0:T(1024)S(1)} %copy-done.34, f32[768]{0:T(1024)S(1)} %copy-done.33, ...), kind=kOutput, calls=%fused_computation.143 | convolution fusion | flops 5043388416 | bytes 39348224 | tf_op jit(solution)/shard_map/dot_general | solution.py:166
  704.3 21.4 all_gather.7
  753.6 23.1 reduce-scatter.5.cloned.1.call-done
  798.6 18.9 convert_reduce_fusion
  853.0 1276.9 %while.31 = (s32[]{:T(128)}, bf16[2,512,2304]{2,1,0:T(8,128)(2,1)}, f32[2,12,128]{2,1,0:T(8,128)}, bf16[2,512,2304]{1,2,0:T(8,128)(2,1)}, s32[2,512]{1,0:T(2,128...) while((s32[]{:T(128)}, bf16[2,512,2304]{2,1,0:T(8,128)(2,1)}, ...), condition=%wide.region_15.16_spmd, body=%wide.region_13.15_spmd.sunk | while | flops 7732635136 | bytes 323633472 | solution.py:255
  861.2 120.0 %fusion.281 = f32[12,512,512]{2,0,1:T(8,128)} fusion(s32[512,512]{1,0:T(8,128)S(1)} %fusion.280, s32[512,512]{1,0:T(8,128)S(1)} %add_select_fusion.15, f32[12,128]{1,0:T(8,128)} %get-tuple-element.641, bf16[12,128]{1,0:T(8,128)(2,1)} %get-tuple-element.640), kind=kOutput, calls=%fused_computation.62.clone.1 | convolution fusion | flops 905974272 | bytes 14689280 | tf_op jit(solution)/shard_map/while/body/eval_jaxpr/ijb,hb->hij/dot_general | solution.py:58
  981.2 17.8 copy.101
  999.0 120.6 %fusion.282 = f32[512,512,12]{1,2,0:T(8,128)} fusion(s32[512,512]{1,0:T(8,128)} %copy-done.9, s32[512,512]{1,0:T(8,128)} %copy-done.10, bf16[12,128]{1,0:T(8,128)(2,1)} %get-tuple-element.640), kind=kOutput, calls=%fused_computation.63.clone.1 | convolution fusion | flops 905969664 | bytes 14683136 | tf_op jit(solution)/shard_map/while/body/eval_jaxpr/ijb,hb->hij/dot_general | solution.py:55
  1235.9 120.4 %fusion.287 = f32[12,128]{1,0:T(8,128)} fusion(bf16[12,512,512]{2,0,1:T(8,128)(2,1)} %copy.104, s32[512,512]{1,0:T(8,128)} %copy-done.9, s32[512,512]{1,0:T(8,128)} %copy-done.10), kind=kOutput, calls=%fused_computation.88.clone.2 | convolution fusion | flops 905969664 | bytes 8394752 | tf_op jit(solution)/shard_map/while/body/eval_jaxpr/hij,ijb->hb/dot_general | solution.py:104
  1370.8 120.6 %fusion.288 = f32[2,12,128]{2,1,0:T(8,128)} fusion(f32[2,12,128]{2,1,0:T(8,128)} %get-tuple-element.621, s32[]{:T(128)S(6)} %copy.122, f32[12,128]{1,0:T(8,128)} %fusion.287, bf16[12,512,512]{2,0,1:T(8,128)(2,1)} %copy.105, s32[512,512]{1,0:T(8,128)} %copy-done.9, s32[512,512]{1,0:T(8,128)} %copy-done.10), kind=kOutput, calls=%fused_computation.92.clone.2 | convolution fusion | flops 905971200 | bytes 10502148 | tf_op jit(solution)/shard_map/while/body/eval_jaxpr/hij,ijb->hb/dot_general | solution.py:107
  1499.6 120.0 %fusion.281 = f32[12,512,512]{2,0,1:T(8,128)} fusion(s32[512,512]{1,0:T(8,128)S(1)} %fusion.280, s32[512,512]{1,0:T(8,128)S(1)} %add_select_fusion.15, f32[12,128]{1,0:T(8,128)} %get-tuple-element.641, bf16[12,128]{1,0:T(8,128)(2,1)} %get-tuple-element.640), kind=kOutput, calls=%fused_computation.62.clone.1 | convolution fusion | flops 905974272 | bytes 14689280 | tf_op jit(solution)/shard_map/while/body/eval_jaxpr/ijb,hb->hij/dot_general | solution.py:58
  1619.6 17.8 copy.101
  1637.4 120.6 %fusion.282 = f32[512,512,12]{1,2,0:T(8,128)} fusion(s32[512,512]{1,0:T(8,128)} %copy-done.9, s32[512,512]{1,0:T(8,128)} %copy-done.10, bf16[12,128]{1,0:T(8,128)(2,1)} %get-tuple-element.640), kind=kOutput, calls=%fused_computation.63.clone.1 | convolution fusion | flops 905969664 | bytes 14683136 | tf_op jit(solution)/shard_map/while/body/eval_jaxpr/ijb,hb->hij/dot_general | solution.py:55
  1874.2 120.4 %fusion.287 = f32[12,128]{1,0:T(8,128)} fusion(bf16[12,512,512]{2,0,1:T(8,128)(2,1)} %copy.104, s32[512,512]{1,0:T(8,128)} %copy-done.9, s32[512,512]{1,0:T(8,128)} %copy-done.10), kind=kOutput, calls=%fused_computation.88.clone.2 | convolution fusion | flops 905969664 | bytes 8394752 | tf_op jit(solution)/shard_map/while/body/eval_jaxpr/hij,ijb->hb/dot_general | solution.py:104
  2009.2 120.6 %fusion.288 = f32[2,12,128]{2,1,0:T(8,128)} fusion(f32[2,12,128]{2,1,0:T(8,128)} %get-tuple-element.621, s32[]{:T(128)S(6)} %copy.122, f32[12,128]{1,0:T(8,128)} %fusion.287, bf16[12,512,512]{2,0,1:T(8,128)(2,1)} %copy.105, s32[512,512]{1,0:T(8,128)} %copy-done.9, s32[512,512]{1,0:T(8,128)} %copy-done.10), kind=kOutput, calls=%fused_computation.92.clone.2 | convolution fusion | flops 905971200 | bytes 10502148 | tf_op jit(solution)/shard_map/while/body/eval_jaxpr/hij,ijb->hb/dot_general | solution.py:107
  2198.7 42.1 %all-reduce.6 = (f32[768]{0:T(1024)}, f32[768]{0:T(1024)}, f32[768]{0:T(1024)}, f32[768]{0:T(1024)}, f32[3072]{0:T(1024)}, /*index=5*/f32[12,128]{1,0:T(8,128)}) all-reduce(f32[768]{0:T(1024)} %get-tuple-element.355, f32[768]{0:T(1024)} %get-tuple-element.358, ...), channel_id=1, replica_groups=mesh['rows'=2,'gr'=4,'gc'=4] {'rows','gr','gc'}, use_global_device_ids=true, to_apply=%region_19.20 | all-reduce | flops 7680 | bytes 61440 | tf_op jit(solution)/shard_map/psum | solution.py:275
  2246.7 438.6 %all-reduce.10.cloned.1.call-done = (f32[1769472]{0:T(1024)}, f32[589824]{0:T(1024)}, f32[2359296]{0:T(1024)}, f32[2359296]{0:T(1024)}, f32[589824]{0:T(1024)}, /*index=5*/f32[589824]{0:T(1024)}) async-done(((f32[1769472]{0:T(1024)}, f32[589824]{0:T(1024)}, f32[2359296]{0:T(1024)}, f32[2359296]{0:T(1024)}, f32[589824]{0:T(1024)}, /*index=5*/f32[589824]{0:T(1024)}), (f32[1769472]{0:T(1024)}, ...) | async-done | bytes 33030160
  (277 shorter events, 591.8 us)
Async XLA Ops:
  7.2 743.7 %reduce-scatter.3.cloned.1.call-start = ((), (), s32[]{:S(2)}) async-start(), calls=%async_computation.2 | async-start | bytes 983040 | tf_op jit(solution)/shard_map/reduce_scatter | solution.py:202
  9.1 10.5 copy-start.26
  308.4 15.7 copy-start.4
  623.2 15.7 copy-start.4
  657.6 40.5 %slice-start.2 = ((s8[4718592]{0:T(1024)(128)(4,1)}), s8[4194304]{0:T(1024)(128)(4,1)S(1)}, s32[]{:S(2)}) async-start(s8[4718592]{0:T(1024)(128)(4,1)} %bitcast.332), calls=%async_computation.7 | async-start | bytes 8388608
  661.6 36.5 %copy-start.6 = (f32[1024,768]{1,0:T(8,128)}, f32[1024,768]{1,0:T(8,128)S(1)}, u32[]{:S(2)}) copy-start(f32[1024,768]{1,0:T(8,128)S(1)} %get-tuple-element.425) | copy-start | bytes 9437188
  663.2 40.0 %copy-start.42 = (f32[2,64]{1,0:T(2,128)}, f32[2,64]{1,0:T(2,128)S(1)}, u32[]{:S(2)}) copy-start(f32[2,64]{1,0:T(2,128)S(1)} %convert_reduce_fusion.2) | copy-start | bytes 1540
  663.2 34.9 %slice-start.3 = ((s8[4718592]{0:T(1024)(128)(4,1)}), s8[524288]{0:T(1024)(128)(4,1)S(1)}, s32[]{:S(2)}) async-start(s8[4718592]{0:T(1024)(128)(4,1)} %bitcast.332), calls=%async_computation.8 | async-start | bytes 1048576
  703.2 22.5 copy-start.48
  703.2 23.4 copy-start.15
  703.2 23.4 copy-start.23
  728.1 48.5 %reduce-scatter.5.cloned.1.call-start = ((), (), s32[]{:S(2)}) async-start(), calls=%async_computation.3 | async-start | bytes 983040 | tf_op jit(solution)/shard_map/reduce_scatter | solution.py:208
  742.4 1943.0 %all-reduce.10.cloned.1.call-start = ((), (), s32[]{:S(2)}) async-start(), calls=%async_computation.4 | async-start | bytes 66060288
  798.6 18.9 copy-start.7
  817.4 9.8 copy-start.39
  833.6 11.6 slice-start.4
  836.5 8.8 copy-start.24
  853.0 1276.9 %copy-start.27 = (f32[1024]{0:T(1024)S(1)}, f32[1024]{0:T(1024)}, u32[]{:S(2)}) copy-start(f32[1024]{0:T(1024)} %copy-done.26) | copy-start | bytes 12292
  853.0 1276.9 %copy-start.29 = (f32[1024]{0:T(1024)S(1)}, f32[1024]{0:T(1024)}, u32[]{:S(2)}) copy-start(f32[1024]{0:T(1024)} %copy-done.28) | copy-start | bytes 12292
  853.0 1277.0 %copy-start.32 = (f32[768]{0:T(1024)S(1)}, f32[768]{0:T(1024)}, u32[]{:S(2)}) copy-start(f32[768]{0:T(1024)} %param.28) | copy-start | bytes 9220
  1140.1 15.2 copy-start.2
  1140.1 15.2 copy-start.3
  1778.5 15.2 copy-start.2
  1778.5 15.2 copy-start.3
  (46 other events, 176.7 us)
Sparse Core Ops, SparseCore 0:
  728.3 22.6 reduce-scatter.2
  753.3 23.2 reduce-scatter.4
  2183.6 501.7 all-reduce.9
where the time goes:
time: 2720 us; the launch traced here: 2700 us
  matrix products  1770 us (65%)
  waiting for transfers between devices  468 us (17%)
  local copies, waits for them, and re-layouts  323 us (12%)
  blocking collectives  72.2 us (3%)
  other arithmetic  57.3 us (2%)
    dot_general x4, matrix products, head_scores(): jnp.einsum('ijb,hb->hij', segment_members, table_high, preferred_element_...  482 us
    dot_general x4, matrix products, head_scores(): jnp.einsum('ijb,hb->hij', segment_members, table_low, preferred_element_t...  480 us
    unnamed x4, waiting for transfers between devices  439 us
    dot_general x2, matrix products, attend_back(): jnp.einsum('hij,ijb->hb', grad_low, segment_members, preferred_element_ty...  241 us
    dot_general x2, matrix products, attend_back(): jnp.einsum('hij,ijb->hb', grad_high, segment_members, preferred_element_t...  241 us
    dot_general x4, local copies, waits for them, and re-layouts, head_scores(): jnp.einsum('ijb,hb->hij', segment_members, table_low, preferred_element_t...  71.1 us
    dot_general x4, local copies, waits for them, and re-layouts, head_scores(): jnp.einsum('ijb,hb->hij', segment_members, table_high, preferred_element_...  70.7 us
    dot_general x4, matrix products, head_scores(): jnp.einsum('ihc,jhc->hij', queries, key_rows, preferred_element_type=jnp....  61.2 us
  transfers between devices with their start and end apart: 3, of which 3 were waited for; matrix products, arithmetic and copies ran while one was open for 1% of the time, Pallas kernels for 0%

commit v1 on v0

v1 whole, which is shorter than its diff:
```python
import functools
import math

import jax
import jax.numpy as jnp
from jax import lax
from jax.experimental import pallas as pl
from jax.experimental.pallas import tpu as pltpu
from jax.sharding import PartitionSpec as P

COORD=1000
SPAN=2*COORD+1
LOG2E=1.4426950408889634
BARRED=-2.0**99
BF=jnp.bfloat16
F32=jnp.float32
NT=(((1,),(1,)),((),()))
NN=(((1,),(0,)),((),()))
def dot(a,b,dims=NN):
    return lax.dot_general(a,b,dims,preferred_element_type=F32)

def whole_and_rest(scaled):
    whole=jnp.floor((scaled+0.5)*(1.0/SPAN))
    return whole, scaled-SPAN*whole

def key_side(low, high, half):
    c=((low+high)>>1).astype(F32)
    return whole_and_rest(c*half)
def query_side(low, high, half):
    c=((low+high)>>1).astype(F32)
    return whole_and_rest((COORD-c)*half)

def hi_lo(v):
    hi=v.astype(BF)
    return hi, (v-hi.astype(F32)).astype(BF)

def fwd_kernel(q_ref,k_ref,v_ref,boxr_ref,boxc_ref,pager_ref,pagec_ref,tab_ref,
               ctx_ref,e_ref,linv_ref,
               ohb_ref,oha_ref,kg_ref,rxy_ref,pg_ref,cx_ref,cy_ref,*,rows):
    length=q_ref.shape[0]
    half=tab_ref.shape[1]//2
    quarter=half//2
    hp=pl.program_id(1)
    lane=lax.broadcasted_iota(jnp.int32,(1,128),1)
    low=lane<64
    @pl.when(hp==0)
    def _():
        bc=boxc_ref[...]
        ax,fax=key_side(bc[:,0:1],bc[:,2:3],half)
        ay,fay=key_side(bc[:,1:2],bc[:,3:4],half)
        bx,fbx=query_side(bc[:,0:1],bc[:,2:3],half)
        by,fby=query_side(bc[:,1:2],bc[:,3:4],half)
        spot=(lane%quarter).astype(F32)
        is_x=(lane%half)<quarter
        oha=jnp.where(jnp.where(is_x,ax,ay)==spot,1.0,0.0)
        ohb=jnp.where(jnp.where(is_x,bx,by)==spot,1.0,0.0)
        ohb_ref[...]=jnp.where(low,ohb,0.0).astype(BF)
        oha_ref[...]=oha.astype(BF)
        page=pagec_ref[...]
        mine=(lane%64)==page
        barred=jnp.where((lane%64)<4,jnp.where(mine,0.0,BARRED),0.0)
        kg_ref[0]=jnp.where(low,oha,barred).astype(BF)
        kg_ref[1]=jnp.where(low,barred,oha).astype(BF)
        pg_ref[...]=jnp.where(mine,1.0,0.0).astype(BF)
        ohx=jnp.where(ax==spot,1.0,0.0)
        ohy=jnp.where(ay==spot,1.0,0.0)
        rxy_ref[pl.ds(0,length),:]=jnp.where(low,ohx,0.0).astype(BF)
        rxy_ref[pl.ds(length,length),:]=jnp.where(low,0.0,ohy).astype(BF)
        br=boxr_ref[...]
        _,gax=key_side(br[0:1],br[2:3],half)
        _,gay=key_side(br[1:2],br[3:4],half)
        cx_ref[...]=jnp.where(gax+fbx>=SPAN,1.0,0.0)
        cy_ref[...]=jnp.where(gay+fby>=SPAN,1.0,0.0)
    k=k_ref[...]
    v=v_ref[...]
    oha=oha_ref[...]
    b_row=lax.broadcasted_iota(jnp.int32,(half,128),0)
    l_col=lax.broadcasted_iota(jnp.int32,(half,128),1)
    row_x=b_row<quarter
    index=jnp.where(row_x,b_row,b_row-quarter+half)+l_col%quarter
    same_axis=row_x==((l_col%half)<quarter)
    d_axis=row_x==(l_col<half)
    heads=[]
    for a in range(2):
        t=jnp.broadcast_to(tab_ref[pl.ds(2*hp+a,1),:],(half,128))
        base=jnp.take_along_axis(t,index,axis=1,mode="promise_in_bounds")
        nxt=jnp.take_along_axis(t,index+1,axis=1,mode="promise_in_bounds")
        hi,lo=hi_lo(base)
        dhi,dlo=hi_lo(nxt-base)
        z=jnp.zeros_like(hi)
        is_hi=(l_col<64)==(a==1)
        g0=jnp.where(same_axis,jnp.where(is_hi,hi.astype(F32),lo.astype(F32)),0.0).astype(BF)
        g1=jnp.where(d_axis,jnp.where((l_col%half)<quarter,dhi.astype(F32),dlo.astype(F32)),0.0).astype(BF)
        hk=jnp.concatenate([g0,g1],axis=1)
        left=dot(ohb_ref[:,0:half],hk).astype(BF)
        if a==0:
            rhs=jnp.concatenate([jnp.where(low,k,oha),kg_ref[0]],axis=1)
            vv=jnp.where(low,v,jnp.ones_like(v))
        else:
            rhs=jnp.concatenate([jnp.where(low,oha,k),kg_ref[1]],axis=1)
            vv=jnp.where(low,jnp.ones_like(v),v)
        heads.append((left,rhs,vv))
    for c in range(length//rows):
        sl=pl.ds(c*rows,rows)
        q=q_ref[sl,:]*jnp.asarray(0.125,BF)
        pg=pg_ref[sl,:]
        outs=[]
        for a in range(2):
            left,rhs,vv=heads[a]
            lc=left[c*rows:(c+1)*rows]
            g0=lc[:,:128]
            if a==0:
                lhs=jnp.concatenate([jnp.where(low,q,g0),jnp.where(low,g0,pg)],axis=1)
            else:
                lhs=jnp.concatenate([jnp.where(low,g0,q),jnp.where(low,pg,g0)],axis=1)
            s=dot(lhs,rhs,NT)
            dxy=dot(lc[:,128:],rxy_ref[...],NT)
            s=s+cx_ref[sl,:]*dxy[:,:length]+cy_ref[sl,:]*dxy[:,length:]
            m=jnp.max(s,axis=1,keepdims=True)
            e=jnp.exp2((s-m)*LOG2E).astype(BF)
            e_ref[a,sl,:]=e
            outs.append(dot(e,vv))
        ctx=jnp.where(low,outs[0],outs[1])
        tot=jnp.where(low,pltpu.roll(outs[0],64,1),pltpu.roll(outs[1],64,1))
        linv=1.0/tot
        linv_ref[sl,:]=linv
        ctx_ref[sl,:]=(ctx*linv).astype(BF)

def attend_forward(qkv,boxes_r,boxes_c,page_r,page_c,table,rows=256):
    tokens,width=qkv.shape
    feats=width//3
    seqs,_,length=page_r.shape
    heads=table.shape[0]
    pairs=heads//2
    return pl.pallas_call(
        functools.partial(fwd_kernel,rows=rows),
        grid=(seqs,pairs),
        in_specs=[
            pl.BlockSpec((length,128),lambda s,h:(s,h)),
            pl.BlockSpec((length,128),lambda s,h:(s,pairs+h)),
            pl.BlockSpec((length,128),lambda s,h:(s,2*pairs+h)),
            pl.BlockSpec((4,length),lambda s,h:(0,s)),
            pl.BlockSpec((length,4),lambda s,h:(s,0)),
            pl.BlockSpec((None,1,length),lambda s,h:(s,0,0)),
            pl.BlockSpec((length,1),lambda s,h:(s,0)),
            pl.BlockSpec(table.shape,lambda s,h:(0,0)),
        ],
        out_specs=[
            pl.BlockSpec((length,128),lambda s,h:(s,h)),
            pl.BlockSpec((2,None,length,length),lambda s,h:(h,s,0,0)),
            pl.BlockSpec((length,128),lambda s,h:(s,h)),
        ],
        out_shape=[jax.ShapeDtypeStruct((tokens,feats),BF),
                   jax.ShapeDtypeStruct((heads,seqs,length,length),BF),
                   jax.ShapeDtypeStruct((tokens,feats),F32)],
        scratch_shapes=[pltpu.VMEM((length,128),BF),pltpu.VMEM((length,128),BF),
                        pltpu.VMEM((2,length,128),BF),pltpu.VMEM((2*length,128),BF),
                        pltpu.VMEM((length,128),BF),
                        pltpu.VMEM((length,length),F32),pltpu.VMEM((length,length),F32)],
        name="attend_forward",
    )(qkv,qkv,qkv,boxes_r,boxes_c,page_r,page_c,table)

def bwd_kernel(q_ref,k_ref,v_ref,e_ref,linv_ref,ctx_ref,gctx_ref,boxr_ref,boxc_ref,
               gq_ref,gk_ref,gv_ref,hist_ref,
               oha_ref,ohbt_ref,cx_ref,cy_ref,g_ref,gx_ref,gy_ref,lt_ref,gt_ref,*,rows):
    length=q_ref.shape[0]
    half=64
    quarter=half//2
    s_id=pl.program_id(0)
    hp=pl.program_id(1)
    lane=lax.broadcasted_iota(jnp.int32,(1,128),1)
    low=lane<64
    @pl.when(hp==0)
    def _():
        bc=boxc_ref[...]
        ax,_=key_side(bc[:,0:1],bc[:,2:3],half)
        ay,_=key_side(bc[:,1:2],bc[:,3:4],half)
        _,fbx=query_side(bc[:,0:1],bc[:,2:3],half)
        _,fby=query_side(bc[:,1:2],bc[:,3:4],half)
        spot=(lane%quarter).astype(F32)
        is_x=(lane%half)<quarter
        oha_ref[...]=jnp.where(jnp.where(is_x,ax,ay)==spot,jnp.where(low,1.0,0.0),0.0).astype(BF)
        br=boxr_ref[...]
        _,gax=key_side(br[0:1],br[2:3],half)
        _,gay=key_side(br[1:2],br[3:4],half)
        rbx,_=query_side(br[0:1],br[2:3],half)
        rby,_=query_side(br[1:2],br[3:4],half)
        row=lax.broadcasted_iota(jnp.int32,(half,length),0)
        rspot=(row%quarter).astype(F32)
        ohbt_ref[...]=jnp.where(jnp.where(row<quarter,rbx,rby)==rspot,1.0,0.0).astype(BF)
        cx_ref[...]=jnp.where(gax+fbx>=SPAN,1.0,0.0).astype(BF)
        cy_ref[...]=jnp.where(gay+fby>=SPAN,1.0,0.0).astype(BF)
    k=k_ref[...]
    v=v_ref[...]
    lt_ref[...]=q_ref[...].astype(F32).T.astype(BF)
    gc=gctx_ref[...].astype(F32)*linv_ref[...]
    gcb=gc.astype(BF)
    gt_ref[...]=gcb.astype(F32).T.astype(BF)
    prod=gc*ctx_ref[...].astype(F32)
    ohbt=ohbt_ref[...]
    kts=[]
    vts=[]
    for a in range(2):
        mine=low if a==0 else jnp.logical_not(low)
        other=64-64*a
        D=jnp.sum(jnp.where(mine,prod,0.0),axis=1,keepdims=True)
        dhi=D.astype(BF).astype(F32)
        dlo=D-dhi
        lhs=jnp.where(mine,gcb.astype(F32),jnp.where(lane==other,dhi,jnp.where(lane==other+1,dlo,0.0))).astype(BF)
        rhs=jnp.where(mine,v,jnp.where((lane==other)|(lane==other+1),-1.0,0.0).astype(BF))
        for c in range(length//rows):
            sl=slice(c*rows,(c+1)*rows)
            gp=dot(lhs[sl],rhs,NT)
            g=(gp*e_ref[a,sl,:].astype(F32)).astype(BF)
            g_ref[a,sl,:]=g
            gx_ref[a,sl,:]=g*cx_ref[sl,:]
            gy_ref[a,sl,:]=g*cy_ref[sl,:]
        left=jnp.concatenate([lt_ref[64*a:64*a+64,:],ohbt],axis=0)
        r0=dot(left,g_ref[a])
        rx=dot(ohbt[:quarter],gx_ref[a])
        ry=dot(ohbt[quarter:],gy_ref[a])
        vts.append(dot(gt_ref[64*a:64*a+64,:],e_ref[a]))
        kts.append(r0[:64])
        w=jnp.concatenate([r0[64:],rx,ry],axis=0)
        whi,wlo=hi_lo(w)
        red=dot(jnp.concatenate([whi,wlo],axis=0),oha_ref[...])
        red=red[:128]+red[128:]
        hist_ref[a]=red
    zero=jnp.zeros_like(k)
    gq=dot(g_ref[0],jnp.where(low,k,zero))+dot(g_ref[1],jnp.where(low,zero,k))
    gq_ref[...]=(gq*0.125).astype(BF)
    gk_ref[...]=(jnp.concatenate(kts,axis=0)*0.125).T.astype(BF)
    gv_ref[...]=jnp.concatenate(vts,axis=0).T.astype(BF)

def attend_backward(qkv,e,linv,ctx,gctx,boxes_r,boxes_c,rows=256):
    tokens,width=qkv.shape
    feats=width//3
    heads,seqs,length,_=e.shape
    pairs=heads//2
    pair=pl.BlockSpec((length,128),lambda s,h:(s,h))
    gq,gk,gv,hist=pl.pallas_call(
        functools.partial(bwd_kernel,rows=rows),
        grid=(seqs,pairs),
        in_specs=[
            pair,
            pl.BlockSpec((length,128),lambda s,h:(s,pairs+h)),
            pl.BlockSpec((length,128),lambda s,h:(s,2*pairs+h)),
            pl.BlockSpec((2,None,length,length),lambda s,h:(h,s,0,0)),
            pair,pair,pair,
            pl.BlockSpec((4,length),lambda s,h:(0,s)),
            pl.BlockSpec((length,4),lambda s,h:(s,0)),
        ],
        out_specs=[pair,pair,pair,pl.BlockSpec((None,2,128,128),lambda s,h:(s,h,0,0))],
        out_shape=[jax.ShapeDtypeStruct((tokens,feats),BF)]*3+[jax.ShapeDtypeStruct((seqs,heads,128,128),F32)],
        scratch_shapes=[pltpu.VMEM((length,128),BF),pltpu.VMEM((64,length),BF),
                        pltpu.VMEM((length,length),BF),pltpu.VMEM((length,length),BF),
                        pltpu.VMEM((2,length,length),BF),pltpu.VMEM((2,length,length),BF),pltpu.VMEM((2,length,length),BF),
                        pltpu.VMEM((128,length),BF),pltpu.VMEM((128,length),BF)],
        name="attend_backward",
    )(qkv,qkv,qkv,e,linv,ctx,gctx,boxes_r,boxes_c)
    return gq,gk,gv,table_gradient(hist)

def table_gradient(hist):
    seqs,heads=hist.shape[:2]
    w=jnp.sum(hist,axis=0)
    quarter=32
    w=w.reshape(heads,2,2,quarter,4,quarter)[:, :, :, :, :2]
    w=jnp.stack([w[:,:,0,:,0],w[:,:,1,:,1]],axis=2)
    plain=w[:,0]-w[:,1]
    carry=w[:,1]
    both=jnp.stack([plain,carry],axis=2).reshape(heads,2,2*quarter*quarter)
    total=lax.iota(jnp.int32,quarter)[:,None]+lax.iota(jnp.int32,quarter)[None,:]
    idx=jnp.stack([total,total+1],0).reshape(-1)
    onehot=(idx[:,None]==lax.iota(jnp.int32,64)[None,:]).astype(F32)
    return jnp.einsum("hak,ke->hae",both,onehot,precision=lax.Precision.HIGHEST).reshape(heads,128)


EPSILON = 1e-05


def norm_stats(rows):
    average = jnp.mean(rows, axis=-1, keepdims=True)
    centred = rows - average
    variance = jnp.mean(centred * centred, axis=-1, keepdims=True)
    return average, lax.rsqrt(variance + EPSILON)


def norm_back(g_out, rows, average, inverse, gain):
    z = (rows - average) * inverse
    g_z = g_out * gain
    grad_in = inverse * (
        g_z
        - jnp.mean(g_z, axis=-1, keepdims=True)
        - z * jnp.mean(g_z * z, axis=-1, keepdims=True)
    )
    return grad_in, jnp.sum(g_out * z, axis=0), jnp.sum(g_out, axis=0)


def gelu_pair(u):
    bell = jnp.exp(u * u * -0.5)
    t = 1.0 / (1.0 + (0.3275911 * math.sqrt(0.5)) * jnp.abs(u))
    series = t * (
        0.254829592
        + t * (-0.284496736 + t * (1.421413741 + t * (-1.453152027 + t * 1.061405429)))
    )
    tail = 0.5 * series * bell
    below = jnp.where(u < 0.0, tail, 1.0 - tail)
    return u * below, below + u * bell * (1.0 / math.sqrt(2.0 * math.pi))


AXES = ("rows", "gr", "gc")


def shares(partial):
    part = lax.psum_scatter(partial.astype(BF), AXES, scatter_dimension=0, tiled=True)
    return part.astype(F32).reshape(-1)


def body(
    tokens, boxes, page_ids, seg_ids, pair_mask, ln1_gain, ln1_bias, query_key_value_weight,
    attention_output_weight, ln2_gain, ln2_bias, up_projection_weight, up_projection_bias,
    down_projection_weight, box_table, rel_left, rel_right, cot_out, cot_logits,
):
    sequences, length = page_ids.shape
    count = sequences * length
    features = tokens.shape[1]
    x = tokens.astype(F32)
    average1, inverse1 = norm_stats(x)
    h1 = ((x - average1) * inverse1 * ln1_gain + ln1_bias).astype(BF)
    qkv = dot(h1, query_key_value_weight).astype(BF)
    boxes_c = boxes.T
    ctx, e, linv = attend_forward(
        qkv, boxes, boxes_c, page_ids[:, None, :], page_ids.reshape(-1, 1), box_table
    )
    r1 = x + dot(ctx, attention_output_weight)
    average2, inverse2 = norm_stats(r1)
    h2 = ((r1 - average2) * inverse2 * ln2_gain + ln2_bias).astype(BF)
    act, slope = gelu_pair(dot(h2, up_projection_weight) + up_projection_bias)
    act = act.astype(BF)
    slope = slope.astype(BF)
    layer_out = (r1 + dot(act, down_projection_weight)).astype(BF)

    slots = 64
    member = seg_ids[:, :, None] == lax.iota(jnp.int32, slots)[None, None, :]
    members = member.astype(BF)
    counts = jnp.sum(member.astype(F32), axis=1)
    pooled = jnp.einsum(
        "stg,std->sgd", members, layer_out.reshape(sequences, length, features),
        preferred_element_type=F32,
    ) / counts[:, :, None]
    embedded = pooled.reshape(sequences * slots, features).astype(BF)
    left = dot(embedded, rel_left).astype(BF)
    right = dot(embedded, rel_right).astype(BF)
    row_side = lax.all_gather(left, "gc", axis=0, tiled=True)
    col_side = lax.all_gather(right, "gr", axis=0, tiled=True)
    pair_scale = 1.0 / math.sqrt(rel_left.shape[1])
    keep = pair_mask[0].astype(F32)
    pair_logits = keep * dot(row_side, col_side, NT) * pair_scale
    g_raw = (cot_logits[0].astype(F32) * pair_scale * keep).astype(BF)
    g_left = lax.psum_scatter(
        dot(g_raw, col_side).astype(BF), "gc", scatter_dimension=0, tiled=True
    )
    g_right = lax.psum_scatter(
        dot(g_raw, row_side, (((0,), (0,)), ((), ()))).astype(BF), "gr",
        scatter_dimension=0, tiled=True,
    )
    TN = (((0,), (0,)), ((), ()))
    grad_rel_left = dot(embedded, g_left, TN)
    grad_rel_right = dot(embedded, g_right, TN)
    left_share = shares(grad_rel_left)
    right_share = shares(grad_rel_right)
    g_emb = dot(g_left, rel_left, NT) + dot(g_right, rel_right, NT)
    g_seg = (g_emb.reshape(sequences, slots, features) / counts[:, :, None])
    seg_hi, seg_lo = hi_lo(g_seg)
    spread = jnp.einsum("stg,sgd->std", members, seg_hi, preferred_element_type=F32) + jnp.einsum(
        "stg,sgd->std", members, seg_lo, preferred_element_type=F32
    )
    g_y = cot_out.astype(F32) + spread.reshape(count, features)
    g_mlp = g_y.astype(BF)
    grad_down = dot(act, g_mlp, TN)
    down_share = shares(grad_down)
    g_u = (dot(g_mlp, down_projection_weight, NT) * slope.astype(F32)).astype(BF)
    grad_up_bias = jnp.sum(g_u.astype(F32), axis=0)
    grad_up = dot(h2, g_u, TN)
    up_share = shares(grad_up)
    g_h2 = dot(g_u, up_projection_weight, NT)
    g_norm2, grad_ln2_gain, grad_ln2_bias = norm_back(g_h2, r1, average2, inverse2, ln2_gain)
    g_r1 = g_y + g_norm2
    g_att = g_r1.astype(BF)
    grad_out = dot(ctx, g_att, TN)
    out_share = shares(grad_out)
    g_ctx = dot(g_att, attention_output_weight, NT).astype(BF)
    g_q, g_k, g_v, grad_table = attend_backward(qkv, e, linv, ctx, g_ctx, boxes, boxes_c)
    g_qkv = jnp.concatenate([g_q, g_k, g_v], axis=1)
    grad_qkv = dot(h1, g_qkv, TN)
    qkv_share = shares(grad_qkv)
    g_h1 = dot(g_qkv, query_key_value_weight, NT)
    g_norm1, grad_ln1_gain, grad_ln1_bias = norm_back(g_h1, x, average1, inverse1, ln1_gain)
    grad_tokens = g_r1 + g_norm1
    small = lax.psum(
        (grad_ln1_gain, grad_ln1_bias, grad_ln2_gain, grad_ln2_bias, grad_up_bias, grad_table), AXES
    )
    return (
        layer_out, pair_logits[None], grad_tokens, small[0], small[1], qkv_share, out_share,
        small[2], small[3], up_share, small[4], down_share, small[5], left_share, right_share,
    )


def solution(mesh):
    whole = P(AXES, None)
    tile = P("rows", "gr", "gc")
    flat = P(AXES)
    one = P()
    in_specs = (
        whole, P(None, AXES), whole, whole, tile, one, one, one, one, one, one, one, one, one, one,
        one, one, whole, tile,
    )
    out_specs = (
        whole, tile, whole, one, one, flat, flat, one, one, flat, one, flat, one, flat, flat,
    )
    return jax.shard_map(body, mesh=mesh, in_specs=in_specs, out_specs=out_specs, check_vma=False)
```

time: 2720 us -> 816 us (0.30)
  matrix products: 1770 us -> 128 us
  local copies, waits for them, and re-layouts: 323 us -> 34.9 us
  Pallas kernels: 0 us -> 60 us
  other arithmetic: 57.3 us -> 21.5 us
    dot_general x46 -> x25, matrix products: 1730 us -> 128 us  [the longest x21 124 us: dot(): return lax.dot_general(a, b, dims, preferred_element_type=F32)]
    unnamed x4 -> x8, waiting for transfers between devices: 439 us -> 0.13 us
    reduce_scatter x2 -> x8, waiting for transfers between devices: 29 us -> 466 us  [the longest x6 443 us: shares(): lax.psum_scatter(partial.astype(BF), AXES, scatter_dimension=0, tiled=True)]
    dot_general x8 -> x1, local copies, waits for them, and re-layouts: 142 us -> 0.01 us  [table_gradient(): jnp.einsum('hak,ke->hae', both, onehot, precision=lax.Precision.HIGHEST)]
    pallas_call x0 -> x2, Pallas kernels: none -> 60 us  [the longest x1 33.2 us: attend_forward(): pl.pallas_call(functools.partial(fwd_kernel, rows=rows), grid=(seqs, pair...]
    convert_element_type x4 -> x0, local copies, waits for them, and re-layouts: 57.9 us -> none  [the longest x2 28.9 us: split_parts(): high_part = values_in.astype(jnp.bfloat16)]
    sub x2 -> x0, matrix products: 35.3 us -> none  [attend_back(): grad_probs - jnp.sum(softmax_full * grad_probs, axis=-1, keepdims=True)]
  transfers between devices with their start and end apart: 3 -> 8, of which waited for: 3 -> 6; matrix products, arithmetic and copies ran while one was open for 1% -> 16% of each run, Pallas kernels for 0% -> 3%
where the time goes in v1:
time: 816 us; the launch traced here: 807 us
  waiting for transfers between devices  466 us (57%)
  matrix products  128 us (16%)
  blocking collectives  81 us (10%)
  Pallas kernels  60 us (7%)
  local copies, waits for them, and re-layouts  34.9 us (4%)
  other arithmetic  21.5 us (3%)
  between operations  15.2 us (2%)
    reduce_scatter x6, waiting for transfers between devices, shares(): lax.psum_scatter(partial.astype(BF), AXES, scatter_dimension=0, tiled=True)  443 us
    dot_general x21, matrix products, dot(): return lax.dot_general(a, b, dims, preferred_element_type=F32)  124 us
    psum x1, blocking collectives, body(): lax.psum((grad_ln1_gain, grad_ln1_bias, grad_ln2_gain, grad_ln2_bias, gra...  40.8 us
    pallas_call x1, Pallas kernels, attend_forward(): pl.pallas_call(functools.partial(fwd_kernel, rows=rows), grid=(seqs, pair...  33.2 us
    all_gather x1, blocking collectives, body(): col_side = lax.all_gather(right, 'gr', axis=0, tiled=True)  30 us
    pallas_call x1, Pallas kernels, attend_backward(): pl.pallas_call(functools.partial(bwd_kernel, rows=rows), grid=(seqs, pair...  26.8 us
    reduce_scatter x1, waiting for transfers between devices, body(): lax.psum_scatter(dot(g_raw, col_side).astype(BF), 'gc', scatter_dimension...  22.7 us
  transfers between devices with their start and end apart: 8, of which 6 were waited for; matrix products, arithmetic and copies ran while one was open for 16% of the time, Pallas kernels for 3%

profile of v1, /device:TPU:0, one launch (start us, length us, event | category | flops | bytes accessed | tf_op | source)
XLA Modules:
  0.0 806.9 jit_solution(2986289100304921443)
XLA Ops:
  19.0 7.9 convolution_convert_fusion.q_ref.k_ref.v_ref
  26.9 33.2 %attend_forward.1 = (bf16[1024,768]{1,0:T(8,128)(2,1)}, bf16[12,2,512,512]{3,2,1,0:T(8,128)(2,1)}, f32[1024,768]{1,0:T(8,128)}) custom-call(bf16[1024,2304]{1,0:T(8,128)(2,1)} %convolution_convert_fusion.q_ref.k_ref.v_ref, bf16[1024,2304]{1,0:T(8,128)(2,1)} %convolution_convert_fusion.q_ref.k_ref.v_ref, ...), custom_call_target="tpu_custom_call" | custom-call | tf_op jit(solution)/shard_map/attend_forward/pallas_call | solution.py:135
  60.1 3.9 fusion.43
  64.8 17.1 %multiply_convert_fusion.1 = (bf16[1024,3072]{1,0:T(8,128)(2,1)S(1)}, f32[1024,3072]{1,0:T(8,128)}) fusion(f32[3072]{0:T(1024)S(1)} %copy-done.33, bf16[768,3072]{1,0:T(8,128)(2,1)S(1)} %bitcast.103, f32[1024,768]{1,0:T(8,128)S(1)} %get-tuple-element.48, f32[768]{0:T(1024)S(1)} %copy-done.36, f32[768]{0:T(1024)S(1)} %copy-done.30, ...), kind=kOutput, calls=%fused_computation.4 | convolution fusion | flops 4908122112 | bytes 26765312 | tf_op jit(solution)/shard_map/dot_general | solution.py:20
  82.0 5.0 add_convert_fusion.1
  88.2 10.2 %all_gather.6 = bf16[512,768]{1,0:T(8,128)(2,1)S(1)} all-gather(bf16[128,768]{1,0:T(8,128)(2,1)S(1)} %convolution_convert_fusion.11), channel_id=1, replica_groups=mesh['rows'=2,'gr'=4,'gc'=4] {'gc'}, dimensions={0}, use_global_device_ids=true | all-gather | bytes 983040 | tf_op jit(solution)/shard_map/all_gather | solution.py:354
  102.7 30.0 %all_gather.7 = bf16[512,768]{1,0:T(8,128)(2,1)S(1)} all-gather(bf16[128,768]{1,0:T(8,128)(2,1)S(1)} %convolution_convert_fusion.10), channel_id=1, replica_groups=mesh['rows'=2,'gr'=4,'gc'=4] {'gr'}, dimensions={0}, use_global_device_ids=true | all-gather | bytes 983040 | tf_op jit(solution)/shard_map/all_gather | solution.py:355
  138.9 22.7 %reduce-scatter.9.cloned.1.call-done = bf16[128,768]{1,0:T(8,128)(2,1)} async-done(((bf16[512,768]{1,0:T(8,128)(2,1)}), bf16[128,768]{1,0:T(8,128)(2,1)}) %reduce-scatter.9.cloned.1.call-update) | async-done | bytes 196624 | tf_op jit(solution)/shard_map/reduce_scatter | solution.py:360
  173.9 20.0 %convert_reduce_fusion = (f32[3072]{0:T(1024)}, bf16[1024,3072]{1,0:T(8,128)(2,1)}) fusion(f32[1024,3072]{1,0:T(8,128)} %get-tuple-element.50, f32[3072]{0:T(1024)S(1)} %copy-done.34, bf16[1024,768]{1,0:T(8,128)(2,1)S(1)} %fusion.14, bf16[3072,768]{1,0:T(8,128)(2,1)} %param.32), kind=kOutput, calls=%fused_computation.1 | convolution fusion | flops 4926206976 | bytes 25190400 | tf_op jit(solution)/shard_map/dot_general | solution.py:20
  193.9 8.8 %multiply_reduce_fusion = (f32[768]{0:T(1024)}, f32[1024]{0:T(1024)S(1)}, f32[1024]{0:T(1024)S(1)}, f32[768]{0:T(1024)}, f32[1024,768]{1,0:T(8,128)S(1)}) fusion(f32[1024,768]{1,0:T(8,128)S(1)} %copy-done.4, f32[1024]{0:T(1024)S(1)} %add_rsqrt_fusion, f32[1024]{0:T(1024)S(1)} %broadcast_multiply_fusion.4, f32[768]{0:T(1024)S(1)} %copy-done.31, ...), kind=kOutput, calls=%fused_computation.29 | convolution fusion | flops 4838912000 | bytes 17327104 | tf_op jit(solution)/shard_map/dot_general | solution.py:20
  208.7 4.8 convolution_convert_fusion.4.gctx_ref
  213.5 26.8 %attend_backward.1 = (bf16[1024,768]{1,0:T(8,128)(2,1)}, bf16[1024,768]{1,0:T(8,128)(2,1)}, bf16[1024,768]{1,0:T(8,128)(2,1)}, f32[2,12,128,128]{3,2,1,0:T(8,128)}) custom-call(bf16[1024,2304]{1,0:T(8,128)(2,1)} %convolution_convert_fusion.q_ref.k_ref.v_ref, bf16[1024,2304]{1,0:T(8,128)(2,1)} %convolution_convert_fusion.q_ref.k_ref.v_ref, ...), custom_call_target="tpu_custom_call" | custom-call | tf_op jit(solution)/shard_map/attend_backward/pallas_call | solution.py:241
  245.1 5.7 convolution_convert_fusion.3
  251.5 10.5 %convolution_convert_fusion.2 = bf16[768,3072]{1,0:T(8,128)(2,1)} fusion(bf16[1024,3072]{1,0:T(8,128)(2,1)} %get-tuple-element.54, f32[1024,768]{1,0:T(8,128)} %copy-done.3, f32[768]{0:T(1024)} %param.29, f32[768]{0:T(1024)S(1)} %copy-done.32, f32[1024]{0:T(1024)S(1)} %copy-done.27, f32[1024]{0:T(1024)S(1)} %broadcast_multiply_fusion.4), kind=kOutput, calls=%fused_computation.9 | convolution fusion | flops 4838129664 | bytes 14170112 | tf_op jit(solution)/shard_map/dot_general | solution.py:20
  262.0 9.5 %convolution_convert_fusion.1 = bf16[3072,768]{1,0:T(8,128)(2,1)} fusion(bf16[1024,3072]{1,0:T(8,128)(2,1)} %copy-done.38, bf16[1024,768]{1,0:T(8,128)(2,1)} %copy-done.16), kind=kOutput, calls=%fused_computation.8 | convolution fusion | flops 4834197504 | bytes 12582912 | tf_op jit(solution)/shard_map/dot_general | solution.py:20
  278.8 3.6 reshape.196
  290.5 9.4 %fusion.12 = (f32[768]{0:T(1024)}, f32[1024]{0:T(1024)}, f32[1024]{0:T(1024)}, f32[768]{0:T(1024)}, f32[1024,768]{1,0:T(8,128)}) fusion(bf16[1024,768]{1,0:T(8,128)(2,1)} %param.19, f32[1024]{0:T(1024)} %add_rsqrt_fusion.1, f32[1024]{0:T(1024)S(1)} %copy-done.21, f32[768]{0:T(1024)} %param.24, bf16[1024,2304]{1,0:T(8,128)(2,1)} %copy-done.18, ...), kind=kOutput, calls=%fused_computation.26 | convolution fusion | flops 3631739392 | bytes 13001728 | tf_op jit(solution)/shard_map/dot_general | solution.py:20
  299.9 40.8 %all-reduce = (f32[768]{0:T(1024)}, f32[768]{0:T(1024)}, f32[768]{0:T(1024)}, f32[768]{0:T(1024)}, f32[3072]{0:T(1024)}, /*index=5*/f32[12,128]{1,0:T(8,128)}) all-reduce(f32[768]{0:T(1024)} %get-tuple-element.31, f32[768]{0:T(1024)} %get-tuple-element.36, ...), channel_id=1, replica_groups=mesh['rows'=2,'gr'=4,'gc'=4] {'rows','gr','gc'}, use_global_device_ids=true, to_apply=%region_12.13 | all-reduce | flops 7680 | bytes 61440 | tf_op jit(solution)/shard_map/psum | solution.py:400
  342.1 5.1 fusion.11
  348.7 16.0 %reduce-scatter.21.cloned.1.call-done = bf16[24,768]{1,0:T(8,128)(2,1)} async-done(((bf16[768,768]{1,0:T(8,128)(2,1)}), bf16[24,768]{1,0:T(8,128)(2,1)}) %reduce-scatter.21.cloned.1.call-update) | async-done | bytes 36880 | tf_op jit(solution)/shard_map/reduce_scatter | solution.py:315
  366.2 99.6 %reduce-scatter.15.cloned.1.call-done = bf16[24,768]{1,0:T(8,128)(2,1)} async-done(((bf16[768,768]{1,0:T(8,128)(2,1)}), bf16[24,768]{1,0:T(8,128)(2,1)}) %reduce-scatter.15.cloned.1.call-update) | async-done | bytes 36880 | tf_op jit(solution)/shard_map/reduce_scatter | solution.py:315
  467.2 106.7 %reduce-scatter.13.cloned.1.call-done = bf16[24,2304]{1,0:T(8,128)(2,1)} async-done(((bf16[768,2304]{1,0:T(8,128)(2,1)}), bf16[24,2304]{1,0:T(8,128)(2,1)}) %reduce-scatter.13.cloned.1.call-update) | async-done | bytes 110608 | tf_op jit(solution)/shard_map/reduce_scatter | solution.py:315
  575.6 110.6 %reduce-scatter.17.cloned.1.call-done = bf16[24,3072]{1,0:T(8,128)(2,1)} async-done(((bf16[768,3072]{1,0:T(8,128)(2,1)}), bf16[24,3072]{1,0:T(8,128)(2,1)}) %reduce-scatter.17.cloned.1.call-update) | async-done | bytes 147472 | tf_op jit(solution)/shard_map/reduce_scatter | solution.py:315
  688.0 109.9 %reduce-scatter.19.cloned.1.call-done = bf16[96,768]{1,0:T(8,128)(2,1)} async-done(((bf16[3072,768]{1,0:T(8,128)(2,1)}), bf16[96,768]{1,0:T(8,128)(2,1)}) %reduce-scatter.19.cloned.1.call-update) | async-done | bytes 147472 | tf_op jit(solution)/shard_map/reduce_scatter | solution.py:315
  (163 shorter events, 73.9 us)
Async XLA Ops:
  7.2 11.8 %copy-start = (bf16[768,2304]{1,0:T(8,128)(2,1)S(1)}, bf16[768,2304]{1,0:T(8,128)(2,1)}, u32[]{:S(2)}) copy-start(bf16[768,2304]{1,0:T(8,128)(2,1)} %param.26) | copy-start | bytes 10616836
  7.2 10.8 %copy-start.19 = (s32[4,1024]{1,0:T(4,128)S(1)}, s32[4,1024]{1,0:T(4,128)}, u32[]{:S(2)}) copy-start(s32[4,1024]{1,0:T(4,128)} %boxr_ref.3) | copy-start | bytes 49156
  7.2 129.0 %reduce-scatter.11.cloned.1.call-start = ((), (), s32[]{:S(2)}) async-start(), calls=%async_computation.9 | async-start | bytes 983040 | tf_op jit(solution)/shard_map/reduce_scatter | solution.py:363
  64.0 17.9 %copy-start.3 = (f32[1024,768]{1,0:T(8,128)}, f32[1024,768]{1,0:T(8,128)S(1)}, u32[]{:S(2)}) copy-start(f32[1024,768]{1,0:T(8,128)S(1)} %get-tuple-element.48) | copy-start | bytes 9437188
  64.1 17.9 %slice-start = ((s8[4718592]{0:T(1024)(128)(4,1)}), s8[4194304]{0:T(1024)(128)(4,1)S(1)}, s32[]{:S(2)}) async-start(s8[4718592]{0:T(1024)(128)(4,1)} %bitcast.100), calls=%async_computation.16 | async-start | bytes 8388608
  64.8 137.9 %copy-start.26 = (f32[1024]{0:T(1024)}, f32[1024]{0:T(1024)S(1)}, u32[]{:S(2)}) copy-start(f32[1024]{0:T(1024)S(1)} %add_rsqrt_fusion) | copy-start | bytes 12292
  64.8 17.1 %slice-start.1 = ((s8[4718592]{0:T(1024)(128)(4,1)}), s8[524288]{0:T(1024)(128)(4,1)S(1)}, s32[]{:S(2)}) async-start(s8[4718592]{0:T(1024)(128)(4,1)} %bitcast.100), calls=%async_computation.17 | async-start | bytes 1048576
  87.1 11.3 %copy-start.37 = (bf16[1024,768]{1,0:T(8,128)(2,1)}, bf16[1024,768]{1,0:T(8,128)(2,1)S(1)}, u32[]{:S(2)}) copy-start(bf16[1024,768]{1,0:T(8,128)(2,1)S(1)} %add_convert_fusion.1) | copy-start | bytes 4718596
  87.1 12.2 %copy-start.6 = (s32[1,512,512]{2,1,0:T(8,128)S(1)}, s32[1,512,512]{2,1,0:T(8,128)}, u32[]{:S(2)}) copy-start(s32[1,512,512]{2,1,0:T(8,128)} %param.23) | copy-start | bytes 3145732
  87.1 12.2 %copy-start.13 = (bf16[1,512,512]{2,1,0:T(8,128)(2,1)S(1)}, bf16[1,512,512]{2,1,0:T(8,128)(2,1)}, u32[]{:S(2)}) copy-start(bf16[1,512,512]{2,1,0:T(8,128)(2,1)} %param.37) | copy-start | bytes 1572868
  100.8 60.7 %reduce-scatter.9.cloned.1.call-start = ((), (), s32[]{:S(2)}) async-start(), calls=%async_computation.8 | async-start | bytes 983040 | tf_op jit(solution)/shard_map/reduce_scatter | solution.py:360
  100.9 32.7 %copy-start.7 = (s32[1,512,512]{2,1,0:T(8,128)S(1)}, s32[1,512,512]{2,1,0:T(8,128)}, u32[]{:S(2)}) copy-start(s32[1,512,512]{2,1,0:T(8,128)} %param.23) | copy-start | bytes 3145732
  136.1 211.1 %reduce-scatter.23.cloned.1.call-start = ((), (), s32[]{:S(2)}) async-start(), calls=%async_computation.15 | async-start | bytes 1216512 | tf_op jit(solution)/shard_map/reduce_scatter | solution.py:315
  138.8 225.9 %reduce-scatter.21.cloned.1.call-start = ((), (), s32[]{:S(2)}) async-start(), calls=%async_computation.14 | async-start | bytes 1216512 | tf_op jit(solution)/shard_map/reduce_scatter | solution.py:315
  170.9 294.9 %reduce-scatter.15.cloned.1.call-start = ((), (), s32[]{:S(2)}) async-start(), calls=%async_computation.11 | async-start | bytes 1216512 | tf_op jit(solution)/shard_map/reduce_scatter | solution.py:315
  171.0 22.9 %slice-start.4 = ((s8[4718592]{0:T(1024)(128)(4,1)}), s8[4194304]{0:T(1024)(128)(4,1)S(1)}, s32[]{:S(2)}) async-start(s8[4718592]{0:T(1024)(128)(4,1)} %bitcast.104), calls=%async_computation.20 | async-start | bytes 8388608
  173.9 20.0 %copy-start.16 = (bf16[1024,768]{1,0:T(8,128)(2,1)}, bf16[1024,768]{1,0:T(8,128)(2,1)S(1)}, u32[]{:S(2)}) copy-start(bf16[1024,768]{1,0:T(8,128)(2,1)S(1)} %fusion.14) | copy-start | bytes 4718596
  173.9 20.0 %copy-start.4 = (f32[1024,768]{1,0:T(8,128)S(1)}, f32[1024,768]{1,0:T(8,128)}, u32[]{:S(2)}) copy-start(f32[1024,768]{1,0:T(8,128)} %copy-done.3) | copy-start | bytes 9437188
  173.9 20.0 %copy-start.31 = (f32[768]{0:T(1024)S(1)}, f32[768]{0:T(1024)}, u32[]{:S(2)}) copy-start(f32[768]{0:T(1024)} %param.28) | copy-start | bytes 9220
  173.9 20.0 %slice-start.5 = ((s8[4718592]{0:T(1024)(128)(4,1)}), s8[524288]{0:T(1024)(128)(4,1)S(1)}, s32[]{:S(2)}) async-start(s8[4718592]{0:T(1024)(128)(4,1)} %bitcast.104), calls=%async_computation.21 | async-start | bytes 1048576
  208.6 365.3 %reduce-scatter.13.cloned.1.call-start = ((), (), s32[]{:S(2)}) async-start(), calls=%async_computation.10 | async-start | bytes 3649536 | tf_op jit(solution)/shard_map/reduce_scatter | solution.py:315
  250.8 435.5 %reduce-scatter.17.cloned.1.call-start = ((), (), s32[]{:S(2)}) async-start(), calls=%async_computation.12 | async-start | bytes 4866048 | tf_op jit(solution)/shard_map/reduce_scatter | solution.py:315
  262.0 535.9 %reduce-scatter.19.cloned.1.call-start = ((), (), s32[]{:S(2)}) async-start(), calls=%async_computation.13 | async-start | bytes 4866048 | tf_op jit(solution)/shard_map/reduce_scatter | solution.py:315
  290.5 51.6 %copy-start.25 = (f32[1024]{0:T(1024)S(1)}, f32[1024]{0:T(1024)}, u32[]{:S(2)}) copy-start(f32[1024]{0:T(1024)} %add_rsqrt_fusion.1) | copy-start | bytes 12292
  (29 other events, 92.4 us)
Sparse Core Ops, SparseCore 0:
  101.0 33.0 reduce-scatter.10
  137.2 24.2 reduce-scatter.8
  167.4 96.1 reduce-scatter.22
  269.3 95.3 reduce-scatter.20
  370.4 95.2 reduce-scatter.14
  471.9 101.9 reduce-scatter.12
  580.3 105.9 reduce-scatter.16
  691.7 106.0 reduce-scatter.18
